TPU v7x, 32 devices: a whole 2x2x4 slice. The times are simulated.
32 devices in a mesh: dom: 8 (over z, y), hub: 4 (over x, core).
Axes of the slice: x: 2, y: 2, z: 4, core: 2. Of those that a mesh axis runs over, the one named last changes fastest.
Arguments:
- node_feats: bfloat16 [8, 4, 2048, 256], P('dom', 'hub'), may hold values from -6 to 6
- hub_feats: bfloat16 [1024, 256], P('hub'), may hold values from -6 to 6
- w_self: bfloat16 [256, 256], replicated, may hold values from -0.375 to 0.375
- w_neigh: bfloat16 [256, 256], replicated, may hold values from -0.375 to 0.375
- out_bias: float32 [256], replicated, may hold values from -3 to 3
- send_rows: int32 [8, 4, 8, 32], P('dom', 'hub'), may hold values from 0 to 2047, as said below
- send_counts: int32 [8, 4, 8], P('dom', 'hub'), may hold values from 0 to 32, as said below
- local_ids: int32 [8, 4, 16, 3], P('dom', 'hub'), may hold values from 0 to 15
- local_tiles: bfloat16 [8, 4, 16, 3, 128, 128], P('dom', 'hub'), may hold values from -0.5 to 0.5
- halo_ids: int32 [8, 4, 16, 2], P('dom', 'hub'), may hold values from 0 to 1
- halo_tiles: bfloat16 [8, 4, 16, 2, 128, 128], P('dom', 'hub'), may hold values from -0.5 to 0.5
- hub_ids: int32 [8, 4, 16, 2], P('dom', 'hub'), may hold values from 0 to 7
- hub_tiles: bfloat16 [8, 4, 16, 2, 128, 128], P('dom', 'hub'), may hold values from -0.5 to 0.5
- degree: int32 [8, 4, 2048], P('dom', 'hub'), may hold values from 1 to 8
- out_grad: bfloat16 [8, 4, 2048, 256], P('dom', 'hub'), may hold values from -6 to 6
Outputs:
- layer_out: bfloat16 [8, 4, 2048, 256], P('dom', 'hub')
- feats_grad: bfloat16 [8, 4, 2048, 256], P('dom', 'hub')
- grad_self: float32 [256, 256], replicated
- grad_neigh: float32 [256, 256], replicated
- grad_bias: float32 [256], replicated
- hub_grads: float32 [1024, 256], P('hub')
Inputs may be any that keep to these rules, and one draw needn't show every extreme that they name: `send_rows`: entry [p, h, a, s] is a row of partition (p, h) that it sends to partition (a, h) in slot s; only the first send_counts[p, h, a] slots of a list are used. `send_counts`: a partition sends nothing to itself; each partition sends 32 rows to at least one peer and receives 32 rows from at least one peer.
All inputs are finite; a program needn't handle non-finite values.
Results may differ from a plain program's by a relative error of at most 0.0056.
Values may be sent and summed in bfloat16 or wider, within the bound.
A program may use at most 128 MiB of HBM per device.

v0:
```python
import math
import jax
import jax.numpy as jnp
from jax import lax
from jax.sharding import PartitionSpec as P


def block_apply(tile_set, sources):
    return jnp.einsum("bkij,bkjf->bif", tile_set, sources, preferred_element_type=jnp.float32)


def block_spread(tile_set, grad_blocks):
    return jnp.einsum("bkij,bif->bkjf", tile_set, grad_blocks, preferred_element_type=jnp.float32)


def silu_slope(preact):
    sigmoid = jax.nn.sigmoid(preact)
    return sigmoid * (1.0 + preact * (1.0 - sigmoid))


def collect_blocks(pieces, index_table, block_total):
    flat_parts = pieces.reshape(
        pieces.shape[0] * pieces.shape[1], pieces.shape[2] * pieces.shape[3]
    )
    wanted = lax.broadcasted_iota(jnp.int32, (block_total, 1), 0)
    onehot = (index_table.reshape(1, -1) == wanted).astype(jnp.float32)
    return jnp.dot(
        onehot, flat_parts, precision=lax.Precision.HIGHEST, preferred_element_type=jnp.float32
    )


def body(
    node_feats,
    hub_feats,
    w_self,
    w_neigh,
    out_bias,
    send_rows,
    send_counts,
    local_ids,
    local_tiles,
    halo_ids,
    halo_tiles,
    hub_ids,
    hub_tiles,
    degree,
    out_grad,
):
    row_count = node_feats.shape[2]
    feat_width = node_feats.shape[3]
    tile_size = local_tiles.shape[-1]
    block_count = row_count // tile_size
    peer_count = lax.axis_size("dom")
    loop_count = lax.axis_size("hub")
    features = node_feats.reshape(row_count, feat_width)
    send_index = send_rows.reshape(peer_count, -1)
    slot_count = send_index.shape[1]
    send_live = lax.broadcasted_iota(jnp.int32, (peer_count, slot_count), 1) < send_counts.reshape(
        peer_count, 1
    )
    outgoing = jnp.where(send_live[:, :, None], features[send_index], jnp.zeros((), features.dtype))
    halo_rows = lax.all_to_all(outgoing, "dom", split_axis=0, concat_axis=0, tiled=True)
    hub_all = lax.all_gather(hub_feats, "hub", axis=0, tiled=True)
    local_index = local_ids[0, 0]
    local_tile = local_tiles[0, 0]
    halo_index = halo_ids[0, 0]
    halo_tile = halo_tiles[0, 0]
    hub_index = hub_ids[0, 0]
    hub_tile = hub_tiles[0, 0]
    summed = block_apply(
        local_tile, features.reshape(block_count, tile_size, feat_width)[local_index]
    )
    summed = summed + block_apply(
        halo_tile, halo_rows.reshape(-1, tile_size, feat_width)[halo_index]
    )
    summed = summed + block_apply(hub_tile, hub_all.reshape(-1, tile_size, feat_width)[hub_index])
    row_scale = 1.0 / degree.reshape(row_count).astype(jnp.float32)
    aggregate = (summed.reshape(row_count, feat_width) * row_scale[:, None]).astype(jnp.bfloat16)
    preact = (
        jnp.dot(features, w_self, preferred_element_type=jnp.float32)
        + jnp.dot(aggregate, w_neigh, preferred_element_type=jnp.float32)
        + out_bias
    )
    layer_rows = jax.nn.silu(preact).astype(jnp.bfloat16)
    grad_pre = (
        out_grad.reshape(row_count, feat_width).astype(jnp.float32) * silu_slope(preact)
    ).astype(jnp.bfloat16)
    contract_rows = (((0,), (0,)), ((), ()))
    contract_cols = (((1,), (1,)), ((), ()))
    part_self = lax.dot_general(
        features, grad_pre, contract_rows, preferred_element_type=jnp.float32
    )
    part_neigh = lax.dot_general(
        aggregate, grad_pre, contract_rows, preferred_element_type=jnp.float32
    )
    part_bias = jnp.sum(grad_pre.astype(jnp.float32), axis=0)
    total_self, total_neigh, total_bias = lax.psum(
        (part_self, part_neigh, part_bias), ("dom", "hub")
    )
    factor = 1.0 / math.sqrt(row_count * peer_count * loop_count)
    direct = lax.dot_general(grad_pre, w_self, contract_cols, preferred_element_type=jnp.float32)
    grad_scaled = lax.dot_general(
        grad_pre, w_neigh, contract_cols, preferred_element_type=jnp.float32
    )
    grad_scaled = (
        (grad_scaled * row_scale[:, None])
        .astype(jnp.bfloat16)
        .reshape(block_count, tile_size, feat_width)
    )
    halo_back = collect_blocks(
        block_spread(halo_tile, grad_scaled), halo_index, peer_count * slot_count // tile_size
    )
    returned = lax.all_to_all(
        halo_back.reshape(peer_count, slot_count, feat_width),
        "dom",
        split_axis=0,
        concat_axis=0,
        tiled=True,
    )
    local_back = collect_blocks(block_spread(local_tile, grad_scaled), local_index, block_count)
    own_grad = direct + local_back.reshape(row_count, feat_width)
    returned = jnp.where(send_live[:, :, None], returned, jnp.zeros((), returned.dtype))
    own_grad = own_grad.at[send_index.reshape(-1)].add(returned.reshape(-1, feat_width))
    hub_pieces = block_spread(hub_tile, grad_scaled)
    hub_dev_rows = hub_feats.shape[0]
    own_blocks = hub_dev_rows // tile_size
    full_sum = collect_blocks(hub_pieces, hub_index, own_blocks * loop_count)
    full_sum = lax.psum(full_sum, ("dom", "hub"))
    my_share = lax.dynamic_slice_in_dim(full_sum, lax.axis_index("hub") * own_blocks, own_blocks, 0)
    hub_grads = my_share.reshape(hub_dev_rows, feat_width)
    return (
        layer_rows.reshape(node_feats.shape),
        own_grad.astype(jnp.bfloat16).reshape(node_feats.shape),
        total_self * factor,
        total_neigh * factor,
        total_bias * factor,
        hub_grads,
    )


def solution(mesh):
    placed = (
        P("dom", "hub", None, None),
        P("hub", None),
        P(),
        P(),
        P(),
        P("dom", "hub", None, None),
        P("dom", "hub", None),
        P("dom", "hub", None, None),
        P("dom", "hub", None, None, None, None),
        P("dom", "hub", None, None),
        P("dom", "hub", None, None, None, None),
        P("dom", "hub", None, None),
        P("dom", "hub", None, None, None, None),
        P("dom", "hub", None),
        P("dom", "hub", None, None),
    )
    return jax.shard_map(
        body,
        mesh=mesh,
        in_specs=placed,
        out_specs=(
            P("dom", "hub", None, None),
            P("dom", "hub", None, None),
            P(),
            P(),
            P(),
            P("hub", None),
        ),
        check_vma=False,
    )
```

profile of v0, /device:TPU:0, one launch (start us, length us, event | category | flops | bytes accessed | tf_op | source)
XLA Modules:
  0.0 287.2 jit_solution(3315615849919298533)
XLA Ops:
  8.9 2.3 gather_fusion.1
  12.0 7.3 %all-to-all-start = ((bf16[8,32,256]{2,1,0:T(8,128)(2,1)}), bf16[8,32,256]{2,1,0:T(8,128)(2,1)S(1)}, u32[]{:S(2)}, u32[]{:S(2)}) async-start(bf16[8,32,256]{2,1,0:T(8,128)(2,1)} %broadcast_select_fusion.1), calls=%async_computation | async-start | bytes 262144 | tf_op jit(solution)/shard_map/all_to_all | solution.py:62
  22.6 7.4 %all_gather.3 = bf16[1024,256]{1,0:T(8,128)(2,1)S(1)} all-gather(bf16[256,256]{1,0:T(8,128)(2,1)} %param.16), channel_id=1, replica_groups=mesh['dom'=8,'hub'=4] {'hub'}, dimensions={0}, use_global_device_ids=true | all-gather | bytes 655360 | tf_op jit(solution)/shard_map/all_gather | solution.py:63
  31.7 2.5 gather_fusion
  34.3 4.0 %fusion.5 = f32[16,256,128,1]{1,2,3,0:T(8,128)} fusion(bf16[16,3,128,256]{3,2,1,0:T(8,128)(2,1)} %bitcast.139, bf16[1,1,16,3,128,128]{5,4,3,2,1,0:T(8,128)(2,1)S(1)} %copy-done), kind=kOutput, calls=%fused_computation.23 | convolution fusion | flops 402653184 | bytes 6815744 | tf_op jit(solution)/shard_map/bkij,bkjf->bif/dot_general | solution.py:9
  38.9 2.0 gather_fusion.3
  40.9 2.0 gather_fusion.2
  43.0 2.6 fusion.10
  48.7 2.2 convert_reduce_fusion
  53.8 2.7 convolution_bitcast_fusion.1
  56.6 2.8 convolution_bitcast_fusion.2
  59.4 3.7 %convolution_bitcast_fusion = f32[16,3,128,256]{2,3,1,0:T(8,128)} fusion(bf16[16,128,256,1]{2,1,3,0:T(8,128)(2,1)S(1)} %bitcast.137, bf16[1,1,16,3,128,128]{5,4,3,2,1,0:T(8,128)(2,1)S(1)} %copy-done), kind=kOutput, calls=%fused_computation.9 | convolution fusion | flops 402653184 | bytes 8912896 | tf_op jit(solution)/shard_map/bkij,bif->bkjf/dot_general | solution.py:13
  63.1 40.2 %psum.30 = f32[256]{0:T(256)S(1)} all-reduce(f32[256]{0:T(256)S(1)} %get-tuple-element.21), channel_id=1, replica_groups=mesh['dom'=8,'hub'=4] {'dom','hub'}, use_global_device_ids=true, to_apply=%region_4.5 | all-reduce | flops 256 | bytes 2048 | tf_op jit(solution)/shard_map/psum | solution.py:97
  103.3 5.5 %copy.63 = f32[4,8,128,256]{3,1,2,0:T(8,128)} copy(f32[4,8,128,256]{2,3,1,0:T(8,128)} %bitcast.133) | data formatting | bytes 8388608
  108.8 5.5 %copy.62 = f32[4,8,128,256]{3,1,2,0:T(8,128)} copy(f32[4,8,128,256]{2,3,1,0:T(8,128)} %bitcast.132) | data formatting | bytes 8388608
  114.3 3.6 %fusion.17 = f32[2,32768]{1,0:T(2,128)S(1)} fusion(f32[32,32768]{1,0:T(8,128)} %bitcast.134, s32[32]{0:T(128)S(1)} %eq.49), kind=kOutput, calls=%fused_computation.54 | convolution fusion | flops 25165888 | bytes 4456576 | tf_op jit(solution)/shard_map/dot_general | solution.py:27
  118.8 5.3 %all-to-all-start.1 = ((f32[8,32,256]{2,1,0:T(8,128)}), f32[8,32,256]{2,1,0:T(8,128)S(1)}, u32[]{:S(2)}, u32[]{:S(2)}) async-start(f32[8,32,256]{2,1,0:T(8,128)} %reshape.247), calls=%async_computation.1 | async-start | bytes 524288 | tf_op jit(solution)/shard_map/all_to_all | solution.py:113
  124.1 6.6 %copy.61 = f32[6,8,128,256]{3,1,2,0:T(8,128)} copy(f32[6,8,128,256]{2,3,1,0:T(8,128)} %bitcast.129) | data formatting | bytes 12582912
  130.7 4.2 %fusion.13 = f32[16,32768]{1,0:T(8,128)S(1)} fusion(f32[48,32768]{1,0:T(8,128)} %bitcast.130, s32[48]{0:T(128)S(1)} %eq.45), kind=kOutput, calls=%fused_computation.41 | convolution fusion | flops 301990656 | bytes 8388800 | tf_op jit(solution)/shard_map/dot_general | solution.py:27
  136.4 4.6 %fusion.15 = f32[8,32768]{1,0:T(8,128)} fusion(f32[32,32768]{1,0:T(8,128)} %bitcast.131, s32[32]{0:T(128)S(1)} %eq.53), kind=kOutput, calls=%fused_computation.50 | convolution fusion | flops 100663552 | bytes 5243008 | tf_op jit(solution)/shard_map/dot_general | solution.py:27
  142.3 3.4 %convolution_add_fusion = f32[2048,256]{1,0:T(8,128)} fusion(f32[2048,256]{1,0:T(8,128)} %reshape.245, bf16[2048,256]{1,0:T(8,128)(2,1)S(1)} %copy-done.4, bf16[256,256]{1,0:T(8,128)(2,1)S(1)} %copy-done.10), kind=kOutput, calls=%fused_computation.6 | convolution fusion | flops 268959744 | bytes 5373952 | tf_op jit(solution)/shard_map/dot_general | solution.py:101
  146.3 4.7 %scatter_fusion = f32[2048,256]{1,0:T(8,128)} fusion(f32[2048,256]{1,0:T(8,128)} %convolution_add_fusion, s32[256]{0:T(256)S(1)} %bitcast.146, f32[256,256]{1,0:T(8,128)S(1)} %bitcast.142), kind=kCustom, calls=%fused_computation.4 | custom fusion | flops 65536 | bytes 787456 | tf_op jit(solution)/shard_map/scatter-add | solution.py:123
  151.0 2.8 convert_bitcast_fusion
  153.8 121.6 %all-reduce.3.cloned.1.call-done = (f32[256,256]{0,1:T(8,128)}, f32[256,256]{0,1:T(8,128)}, f32[8,32768]{1,0:T(8,128)}) async-done(((f32[256,256]{0,1:T(8,128)}, f32[256,256]{0,1:T(8,128)}, f32[8,32768]{1,0:T(8,128)}), (f32[256,256]{0,1:T(8,128)}, f32[256,256]{0,1:T(8,128)}, f32[8,32768]{1,0:T(8,128)})) %all-reduce.3.cloned.1.call-update) | async-done | bytes 1572880 | tf_op jit(solution)/shard_map/psum | solution.py:97
  (81 shorter events, 23.5 us)
Async XLA Ops:
  7.2 27.1 %copy-start = (bf16[1,1,16,3,128,128]{5,4,3,2,1,0:T(8,128)(2,1)S(1)}, bf16[1,1,16,3,128,128]{5,4,3,2,1,0:T(8,128)(2,1)}, u32[]{:S(2)}) copy-start(bf16[1,1,16,3,128,128]{5,4,3,2,1,0:T(8,128)(2,1)} %param.23) | copy-start | bytes 4718596
  7.2 22.8 %copy-start.2 = (bf16[1,1,2048,256]{3,2,1,0:T(8,128)(2,1)S(1)}, bf16[1,1,2048,256]{3,2,1,0:T(8,128)(2,1)}, u32[]{:S(2)}) copy-start(bf16[1,1,2048,256]{3,2,1,0:T(8,128)(2,1)} %param.15) | copy-start | bytes 3145732
  7.2 22.7 %copy-start.10 = (bf16[256,256]{1,0:T(8,128)(2,1)S(1)}, bf16[256,256]{1,0:T(8,128)(2,1)}, u32[]{:S(2)}) copy-start(bf16[256,256]{1,0:T(8,128)(2,1)} %param.17) | copy-start | bytes 393220
  12.0 29.0 %all-to-all-start = ((bf16[8,32,256]{2,1,0:T(8,128)(2,1)}), bf16[8,32,256]{2,1,0:T(8,128)(2,1)S(1)}, u32[]{:S(2)}, u32[]{:S(2)}) async-start(bf16[8,32,256]{2,1,0:T(8,128)(2,1)} %broadcast_select_fusion.1), calls=%async_computation | async-start | bytes 262144 | tf_op jit(solution)/shard_map/all_to_all | solution.py:62
  34.3 4.0 %copy-start.12 = (s32[1,1,8,32]{3,2,1,0:T(8,128)S(1)}, s32[1,1,8,32]{3,2,1,0:T(8,128)}, u32[]{:S(2)}) copy-start(s32[1,1,8,32]{3,2,1,0:T(8,128)} %param.20) | copy-start | bytes 3076
  34.3 4.1 %copy-start.13 = (s32[1,1,16,3]{2,1,3,0:T(1,128)S(1)}, s32[1,1,16,3]{2,1,3,0:T(1,128)}, u32[]{:S(2)}) copy-start(s32[1,1,16,3]{2,1,3,0:T(1,128)} %param.22) | copy-start | bytes 580
  34.3 4.2 %copy-start.14 = (s32[1,1,16,2]{2,3,1,0:T(2,128)S(1)}, s32[1,1,16,2]{2,3,1,0:T(2,128)}, u32[]{:S(2)}) copy-start(s32[1,1,16,2]{2,3,1,0:T(2,128)} %param.24) | copy-start | bytes 388
  34.3 4.2 %copy-start.15 = (s32[1,1,16,2]{2,3,1,0:T(2,128)S(1)}, s32[1,1,16,2]{2,3,1,0:T(2,128)}, u32[]{:S(2)}) copy-start(s32[1,1,16,2]{2,3,1,0:T(2,128)} %param.26) | copy-start | bytes 388
  42.9 2.6 copy-start.5
  42.9 3.2 %copy-start.6 = (bf16[32,128,256]{2,1,0:T(8,128)(2,1)S(1)}, bf16[32,128,256]{2,1,0:T(8,128)(2,1)}, u32[]{:S(2)}) copy-start(bf16[32,128,256]{2,1,0:T(8,128)(2,1)} %gather_fusion.3) | copy-start | bytes 6291460
  43.0 3.4 %copy-start.7 = (bf16[1,1,16,2,128,128]{5,4,3,2,1,0:T(8,128)(2,1)S(1)}, bf16[1,1,16,2,128,128]{5,4,3,2,1,0:T(8,128)(2,1)}, u32[]{:S(2)}) copy-start(bf16[1,1,16,2,128,128]{5,4,3,2,1,0:T(8,128)(2,1)} %param.27) | copy-start | bytes 3145732
  46.4 1.2 copy-start.16
  47.0 1.7 copy-start.9
  47.0 1.7 copy-start.11
  47.0 1.7 copy-start.17
  50.9 2.4 copy-start.3
  53.8 2.7 copy-start.8
  118.8 27.4 %all-to-all-start.1 = ((f32[8,32,256]{2,1,0:T(8,128)}), f32[8,32,256]{2,1,0:T(8,128)S(1)}, u32[]{:S(2)}, u32[]{:S(2)}) async-start(f32[8,32,256]{2,1,0:T(8,128)} %reshape.247), calls=%async_computation.1 | async-start | bytes 524288 | tf_op jit(solution)/shard_map/all_to_all | solution.py:113
  124.1 151.3 %all-reduce.3.cloned.1.call-start = ((), (), s32[]{:S(2)}) async-start(), calls=%async_computation.2 | async-start | bytes 3145728 | tf_op jit(solution)/shard_map/psum | solution.py:97
  141.0 1.2 copy-start.4
  151.0 129.4 %copy-start.1 = (bf16[1,1,16,3,128,128]{5,4,3,2,1,0:T(8,128)(2,1)S(1)}, bf16[1,1,16,3,128,128]{5,4,3,2,1,0:T(8,128)(2,1)}, u32[]{:S(2)}) copy-start(bf16[1,1,16,3,128,128]{5,4,3,2,1,0:T(8,128)(2,1)} %param.23) | copy-start | bytes 4718596
Sparse Core Ops, SparseCore 0:
  141.2 134.1 all-reduce.2
where the time goes:
time: 288 us; the launch traced here: 287 us
  waiting for transfers between devices  122 us (42%)
  blocking collectives  47.6 us (17%)
  matrix products  39 us (14%)
  local copies, waits for them, and re-layouts  37.5 us (13%)
  other arithmetic  14.7 us (5%)
  between operations  14.2 us (5%)
  starting transfers between devices  12.6 us (4%)
    psum x1, waiting for transfers between devices, body(): lax.psum((part_self, part_neigh, part_bias), ('dom', 'hub'))  122 us
    psum x1, blocking collectives, body(): lax.psum((part_self, part_neigh, part_bias), ('dom', 'hub'))  40.2 us
    unnamed x44, local copies, waits for them, and re-layouts  22.9 us
    dot_general x3, matrix products, collect_blocks(): jnp.dot(onehot, flat_parts, precision=lax.Precision.HIGHEST, preferred_el...  12.4 us
    dot_general x3, matrix products, block_spread(): jnp.einsum('bkij,bif->bkjf', tile_set, grad_blocks, preferred_element_typ...  9.24 us
    all_gather x1, blocking collectives, body(): hub_all = lax.all_gather(hub_feats, 'hub', axis=0, tiled=True)  7.38 us
    all_to_all x1, starting transfers between devices, body(): lax.all_to_all(outgoing, 'dom', split_axis=0, concat_axis=0, tiled=True)  7.28 us
    dot_general x3, matrix products, block_apply(): jnp.einsum('bkij,bkjf->bif', tile_set, sources, preferred_element_type=jn...  7.16 us
  transfers between devices with their start and end apart: 3, of which 1 were waited for; matrix products, arithmetic and copies ran while one was open for 15% of the time, Pallas kernels for 0%

commit v1 on v0

--- a/solution.py
+++ b/solution.py
@@ -60,7 +60,19 @@
     )
     outgoing = jnp.where(send_live[:, :, None], features[send_index], jnp.zeros((), features.dtype))
     halo_rows = lax.all_to_all(outgoing, "dom", split_axis=0, concat_axis=0, tiled=True)
-    hub_all = lax.all_gather(hub_feats, "hub", axis=0, tiled=True)
+    q_n = lax.axis_size("hub")
+    frames = [(j0, (j0 + 1) % q_n) for j0 in range(q_n)]
+    leaves = [(j0, (j0 - 1) % q_n) for j0 in range(q_n)]
+    frame_out, n_now = ([hub_feats], [hub_feats])
+    for _ in range(q_n // 2):
+        frame_out.append(lax.ppermute(frame_out[-1], axis_name="hub", perm=frames))
+    for _ in range((q_n - 1) // 2):
+        n_now.append(lax.ppermute(n_now[-1], axis_name="hub", perm=leaves))
+    hub_all = jnp.roll(
+        jnp.concatenate([*frame_out[::-1], *n_now[1:]], axis=0),
+        (lax.axis_index("hub") - q_n // 2) * hub_feats.shape[0],
+        axis=0,
+    )
     local_index = local_ids[0, 0]
     local_tile = local_tiles[0, 0]
     halo_index = halo_ids[0, 0]

time: 288 us -> 287 us (level)
  blocking collectives: 47.6 us -> 41 us
  matrix products: 39 us -> 44.4 us
    all_gather x1 -> x0, blocking collectives: 7.38 us -> none  [body(): hub_all = lax.all_gather(hub_feats, 'hub', axis=0, tiled=True)]
    dot_general x3, matrix products: 7.16 us -> 11.6 us  [block_apply(): jnp.einsum('bkij,bkjf->bif', tile_set, sources, preferred_element_type=jn...]
    unnamed x44 -> x49, local copies, waits for them, and re-layouts: 22.9 us -> 22 us
  transfers between devices with their start and end apart: 3 -> 6, of which waited for: 1 -> 1; matrix products, arithmetic and copies ran while one was open for 15% -> 18% of each run, Pallas kernels for 0% -> 0%
where the time goes in v1:
time: 287 us; the launch traced here: 286 us
  waiting for transfers between devices  121 us (42%)
  matrix products  44.4 us (15%)
  blocking collectives  41 us (14%)
  local copies, waits for them, and re-layouts  37.3 us (13%)
  starting transfers between devices  14.4 us (5%)
  between operations  14.4 us (5%)
  other arithmetic  14 us (5%)
    psum x1, waiting for transfers between devices, body(): lax.psum((part_self, part_neigh, part_bias), ('dom', 'hub'))  121 us
    psum x1, blocking collectives, body(): lax.psum((part_self, part_neigh, part_bias), ('dom', 'hub'))  41 us
    unnamed x49, local copies, waits for them, and re-layouts  22 us
    dot_general x3, matrix products, collect_blocks(): jnp.dot(onehot, flat_parts, precision=lax.Precision.HIGHEST, preferred_el...  12.4 us
    dot_general x3, matrix products, block_apply(): jnp.einsum('bkij,bkjf->bif', tile_set, sources, preferred_element_type=jn...  11.6 us
    dot_general x3, matrix products, block_spread(): jnp.einsum('bkij,bif->bkjf', tile_set, grad_blocks, preferred_element_typ...  9.26 us
    all_to_all x1, starting transfers between devices, body(): lax.all_to_all(outgoing, 'dom', split_axis=0, concat_axis=0, tiled=True)  6.58 us
  transfers between devices with their start and end apart: 6, of which 1 were waited for; matrix products, arithmetic and copies ran while one was open for 18% of the time, Pallas kernels for 0%

profile of v1, /device:TPU:0, one launch (start us, length us, event | category | flops | bytes accessed | tf_op | source)
XLA Modules:
  0.0 286.4 jit_solution(8674665724046263068)
XLA Ops:
  12.1 2.3 gather_fusion.1
  15.1 6.6 %all-to-all-start = ((bf16[8,32,256]{2,1,0:T(8,128)(2,1)}), bf16[8,32,256]{2,1,0:T(8,128)(2,1)S(1)}, u32[]{:S(2)}, u32[]{:S(2)}) async-start(bf16[8,32,256]{2,1,0:T(8,128)(2,1)} %broadcast_select_fusion.1), calls=%async_computation | async-start | bytes 262144 | tf_op jit(solution)/shard_map/all_to_all | solution.py:62
  24.1 2.7 fusion.22
  26.8 2.5 gather_fusion
  29.3 4.0 %fusion.5 = f32[16,256,128,1]{1,2,3,0:T(8,128)} fusion(bf16[16,3,128,256]{3,2,1,0:T(8,128)(2,1)} %bitcast.139, bf16[1,1,16,3,128,128]{5,4,3,2,1,0:T(8,128)(2,1)S(1)} %copy-done), kind=kOutput, calls=%fused_computation.23 | convolution fusion | flops 402653184 | bytes 6815744 | tf_op jit(solution)/shard_map/bkij,bkjf->bif/dot_general | solution.py:9
  34.1 2.0 gather_fusion.2
  36.2 3.8 %fusion.10 = f32[16,256,128,1]{1,2,3,0:T(8,128)} fusion(bf16[16,2,128,256]{3,2,1,0:T(8,128)(2,1)} %bitcast.140, bf16[1,1,16,2,128,128]{5,4,3,2,1,0:T(8,128)(2,1)} %param.25), kind=kOutput, calls=%fused_computation.29 | convolution fusion | flops 268435456 | bytes 5242880 | tf_op jit(solution)/shard_map/bkij,bkjf->bif/dot_general | solution.py:9
  42.2 3.8 %bitcast_add_fusion = f32[16,256,128]{1,2,0:T(8,128)S(1)} fusion(f32[16,256,128,1]{1,2,3,0:T(8,128)} %fusion.10, f32[16,256,128,1]{1,2,3,0:T(8,128)} %fusion.5, bf16[16,2,128,256]{3,2,1,0:T(8,128)(2,1)} %bitcast.141, bf16[1,1,16,2,128,128]{5,4,3,2,1,0:T(8,128)(2,1)} %param.27), kind=kOutput, calls=%fused_computation.17 | convolution fusion | flops 269484032 | bytes 9437184 | tf_op jit(solution)/shard_map/bkij,bkjf->bif/dot_general | solution.py:9
  47.7 2.2 convert_reduce_fusion
  52.9 2.7 convolution_bitcast_fusion.1
  55.6 2.8 convolution_bitcast_fusion.2
  58.4 3.7 %convolution_bitcast_fusion = f32[16,3,128,256]{2,3,1,0:T(8,128)} fusion(bf16[16,128,256,1]{2,1,3,0:T(8,128)(2,1)S(1)} %bitcast.137, bf16[1,1,16,3,128,128]{5,4,3,2,1,0:T(8,128)(2,1)S(1)} %copy-done), kind=kOutput, calls=%fused_computation.9 | convolution fusion | flops 402653184 | bytes 8912896 | tf_op jit(solution)/shard_map/bkij,bif->bkjf/dot_general | solution.py:13
  62.1 41.0 %psum.30 = f32[256]{0:T(256)S(1)} all-reduce(f32[256]{0:T(256)S(1)} %get-tuple-element.21), channel_id=1, replica_groups=mesh['dom'=8,'hub'=4] {'dom','hub'}, use_global_device_ids=true, to_apply=%region_4.5 | all-reduce | flops 256 | bytes 2048 | tf_op jit(solution)/shard_map/psum | solution.py:109
  103.1 5.5 %copy.63 = f32[4,8,128,256]{3,1,2,0:T(8,128)} copy(f32[4,8,128,256]{2,3,1,0:T(8,128)} %bitcast.133) | data formatting | bytes 8388608
  108.6 5.4 %copy.62 = f32[4,8,128,256]{3,1,2,0:T(8,128)} copy(f32[4,8,128,256]{2,3,1,0:T(8,128)} %bitcast.132) | data formatting | bytes 8388608
  114.0 3.6 %fusion.17 = f32[2,32768]{1,0:T(2,128)S(1)} fusion(f32[32,32768]{1,0:T(8,128)} %bitcast.134, s32[32]{0:T(128)S(1)} %eq.52), kind=kOutput, calls=%fused_computation.62 | convolution fusion | flops 25165888 | bytes 4456576 | tf_op jit(solution)/shard_map/dot_general | solution.py:27
  118.6 5.3 %all-to-all-start.1 = ((f32[8,32,256]{2,1,0:T(8,128)}), f32[8,32,256]{2,1,0:T(8,128)S(1)}, u32[]{:S(2)}, u32[]{:S(2)}) async-start(f32[8,32,256]{2,1,0:T(8,128)} %reshape.247), calls=%async_computation.1 | async-start | bytes 524288 | tf_op jit(solution)/shard_map/all_to_all | solution.py:125
  123.9 6.6 %copy.61 = f32[6,8,128,256]{3,1,2,0:T(8,128)} copy(f32[6,8,128,256]{2,3,1,0:T(8,128)} %bitcast.129) | data formatting | bytes 12582912
  130.5 4.2 %fusion.13 = f32[16,32768]{1,0:T(8,128)S(1)} fusion(f32[48,32768]{1,0:T(8,128)} %bitcast.130, s32[48]{0:T(128)S(1)} %eq.48), kind=kOutput, calls=%fused_computation.49 | convolution fusion | flops 301990656 | bytes 8388800 | tf_op jit(solution)/shard_map/dot_general | solution.py:27
  136.2 4.6 %fusion.15 = f32[8,32768]{1,0:T(8,128)} fusion(f32[32,32768]{1,0:T(8,128)} %bitcast.131, s32[32]{0:T(128)S(1)} %eq.56), kind=kOutput, calls=%fused_computation.58 | convolution fusion | flops 100663552 | bytes 5243008 | tf_op jit(solution)/shard_map/dot_general | solution.py:27
  142.0 3.4 %convolution_add_fusion = f32[2048,256]{1,0:T(8,128)} fusion(f32[2048,256]{1,0:T(8,128)} %reshape.245, bf16[2048,256]{1,0:T(8,128)(2,1)S(1)} %copy-done.4, bf16[256,256]{1,0:T(8,128)(2,1)S(1)} %copy-done.9), kind=kOutput, calls=%fused_computation.6 | convolution fusion | flops 268959744 | bytes 5373952 | tf_op jit(solution)/shard_map/dot_general | solution.py:113
  146.1 4.8 %scatter_fusion = f32[2048,256]{1,0:T(8,128)} fusion(f32[2048,256]{1,0:T(8,128)} %convolution_add_fusion, s32[256]{0:T(256)S(1)} %bitcast.146, f32[256,256]{1,0:T(8,128)S(1)} %bitcast.142), kind=kCustom, calls=%fused_computation.4 | custom fusion | flops 65536 | bytes 787456 | tf_op jit(solution)/shard_map/scatter-add | solution.py:135
  150.9 2.8 convert_bitcast_fusion
  153.7 120.8 %all-reduce.3.cloned.1.call-done = (f32[256,256]{0,1:T(8,128)}, f32[256,256]{0,1:T(8,128)}, f32[8,32768]{1,0:T(8,128)}) async-done(((f32[256,256]{0,1:T(8,128)}, f32[256,256]{0,1:T(8,128)}, f32[8,32768]{1,0:T(8,128)}), (f32[256,256]{0,1:T(8,128)}, f32[256,256]{0,1:T(8,128)}, f32[8,32768]{1,0:T(8,128)})) %all-reduce.3.cloned.1.call-update) | async-done | bytes 1572880 | tf_op jit(solution)/shard_map/psum | solution.py:109
  (93 shorter events, 24.7 us)
Async XLA Ops:
  7.2 22.2 %copy-start = (bf16[1,1,16,3,128,128]{5,4,3,2,1,0:T(8,128)(2,1)S(1)}, bf16[1,1,16,3,128,128]{5,4,3,2,1,0:T(8,128)(2,1)}, u32[]{:S(2)}) copy-start(bf16[1,1,16,3,128,128]{5,4,3,2,1,0:T(8,128)(2,1)} %param.23) | copy-start | bytes 4718596
  7.2 16.9 %copy-start.2 = (bf16[1,1,2048,256]{3,2,1,0:T(8,128)(2,1)S(1)}, bf16[1,1,2048,256]{3,2,1,0:T(8,128)(2,1)}, u32[]{:S(2)}) copy-start(bf16[1,1,2048,256]{3,2,1,0:T(8,128)(2,1)} %param.15) | copy-start | bytes 3145732
  7.2 26.8 %collective-permute-start = (bf16[256,256]{1,0:T(8,128)(2,1)}, bf16[256,256]{1,0:T(8,128)(2,1)S(1)}, u32[]{:S(2)}, u32[]{:S(2)}) collective-permute-start(bf16[256,256]{1,0:T(8,128)(2,1)} %param.16), channel_id=1, source_target_pairs={{0,1},{1,2},{2,3},{3,0},{4,5},{5,6},{6,7},{7,4},{8,9},{9,10},{10,1... | collective-permute-start | bytes 393224 | tf_op jit(solution)/shard_map/ppermute | solution.py:68
  7.7 32.3 %collective-permute-start.2 = (bf16[256,256]{1,0:T(8,128)(2,1)}, bf16[256,256]{1,0:T(8,128)(2,1)S(1)}, u32[]{:S(2)}, u32[]{:S(2)}) collective-permute-start(bf16[256,256]{1,0:T(8,128)(2,1)} %param.16), channel_id=1, source_target_pairs={{0,3},{1,0},{2,1},{3,2},{4,7},{5,4},{6,5},{7,6},{8,11},{9,8},{10,9... | collective-permute-start | bytes 393224 | tf_op jit(solution)/shard_map/ppermute | solution.py:70
  15.1 19.0 %all-to-all-start = ((bf16[8,32,256]{2,1,0:T(8,128)(2,1)}), bf16[8,32,256]{2,1,0:T(8,128)(2,1)S(1)}, u32[]{:S(2)}, u32[]{:S(2)}) async-start(bf16[8,32,256]{2,1,0:T(8,128)(2,1)} %broadcast_select_fusion.1), calls=%async_computation | async-start | bytes 262144 | tf_op jit(solution)/shard_map/all_to_all | solution.py:62
  29.3 4.0 %copy-start.13 = (s32[1,1,16,2]{2,3,1,0:T(2,128)S(1)}, s32[1,1,16,2]{2,3,1,0:T(2,128)}, u32[]{:S(2)}) copy-start(s32[1,1,16,2]{2,3,1,0:T(2,128)} %param.24) | copy-start | bytes 388
  29.3 4.0 %copy-start.12 = (s32[1,1,16,3]{2,1,3,0:T(1,128)S(1)}, s32[1,1,16,3]{2,1,3,0:T(1,128)}, u32[]{:S(2)}) copy-start(s32[1,1,16,3]{2,1,3,0:T(1,128)} %param.22) | copy-start | bytes 580
  29.3 4.1 %copy-start.14 = (s32[1,1,16,2]{2,3,1,0:T(2,128)S(1)}, s32[1,1,16,2]{2,3,1,0:T(2,128)}, u32[]{:S(2)}) copy-start(s32[1,1,16,2]{2,3,1,0:T(2,128)} %param.26) | copy-start | bytes 388
  34.0 5.9 %collective-permute-start.1 = (bf16[256,256]{1,0:T(8,128)(2,1)S(1)}, bf16[256,256]{1,0:T(8,128)(2,1)S(1)}, u32[]{:S(2)}, u32[]{:S(2)}) collective-permute-start(bf16[256,256]{1,0:T(8,128)(2,1)S(1)} %collective-permute-done), channel_id=1, source_target_pairs={{0,1},{1,2},{2,3},{3,0},{4,5},{5,6},{6,7},{7,4},{8,9},{9,10},{10,1... | collective-permute-start | bytes 393224 | tf_op jit(solution)/shard_map/ppermute | solution.py:68
  36.2 3.9 %copy-start.8 = (bf16[256,256]{1,0:T(8,128)(2,1)S(1)}, bf16[256,256]{1,0:T(8,128)(2,1)}, u32[]{:S(2)}) copy-start(bf16[256,256]{1,0:T(8,128)(2,1)} %param.16) | copy-start | bytes 393220
  42.2 4.2 %copy-start.15 = (bf16[1,1,2048,256]{3,2,1,0:T(8,128)(2,1)S(1)}, bf16[1,1,2048,256]{3,2,1,0:T(8,128)(2,1)}, u32[]{:S(2)}) copy-start(bf16[1,1,2048,256]{3,2,1,0:T(8,128)(2,1)} %param.29) | copy-start | bytes 3145732
  46.1 1.6 copy-start.7
  46.1 1.6 copy-start.11
  46.1 1.6 copy-start.16
  49.9 2.4 copy-start.3
  51.2 1.7 copy-start.5
  52.8 2.8 copy-start.6
  118.6 27.4 %all-to-all-start.1 = ((f32[8,32,256]{2,1,0:T(8,128)}), f32[8,32,256]{2,1,0:T(8,128)S(1)}, u32[]{:S(2)}, u32[]{:S(2)}) async-start(f32[8,32,256]{2,1,0:T(8,128)} %reshape.247), calls=%async_computation.1 | async-start | bytes 524288 | tf_op jit(solution)/shard_map/all_to_all | solution.py:125
  123.8 150.7 %all-reduce.3.cloned.1.call-start = ((), (), s32[]{:S(2)}) async-start(), calls=%async_computation.2 | async-start | bytes 3145728 | tf_op jit(solution)/shard_map/psum | solution.py:109
  136.2 4.6 %copy-start.9 = (bf16[256,256]{1,0:T(8,128)(2,1)S(1)}, bf16[256,256]{1,0:T(8,128)(2,1)}, u32[]{:S(2)}) copy-start(bf16[256,256]{1,0:T(8,128)(2,1)} %param.17) | copy-start | bytes 393220
  140.8 1.2 copy-start.4
  150.9 128.6 %copy-start.1 = (bf16[1,1,16,3,128,128]{5,4,3,2,1,0:T(8,128)(2,1)S(1)}, bf16[1,1,16,3,128,128]{5,4,3,2,1,0:T(8,128)(2,1)}, u32[]{:S(2)}) copy-start(bf16[1,1,16,3,128,128]{5,4,3,2,1,0:T(8,128)(2,1)} %param.23) | copy-start | bytes 4718596
  274.6 4.1 %copy-start.10 = (f32[256,256]{0,1:T(8,128)S(1)}, f32[256,256]{0,1:T(8,128)}, u32[]{:S(2)}) copy-start(f32[256,256]{0,1:T(8,128)} %get-tuple-element.19) | copy-start | bytes 786436
Sparse Core Ops, SparseCore 0:
  141.0 133.5 all-reduce.2
